TPU v7x, 32 devices: a whole 2x2x4 slice. The times are simulated.
32 devices in a mesh: kvh: 4 (over y, x), seq: 8 (over z, core).
Axes of the slice: x: 2, y: 2, z: 4, core: 2. Of those that a mesh axis runs over, the one named last changes fastest.
Arguments:
- queries: bfloat16 [4, 128, 128], P(None, 'kvh'), may hold values from -256 to 256
- keys: bfloat16 [4, 8, 1024, 128], P(None, 'kvh', 'seq'), may hold values from -6 to 6
- values: bfloat16 [4, 8, 1024, 128], P(None, 'kvh', 'seq'), may hold values from -6 to 6
- lengths: int32 [4, 8], P(None, 'seq'), may hold values from 2 to 128
- hidden_in: bfloat16 [4, 16384], P(None, ('kvh', 'seq')), may hold values from -10 to 10
- out_weight: bfloat16 [16384, 16384], P(('kvh', 'seq')), may hold values from -1 to 1
- norm_gain: bfloat16 [16384], replicated, may hold values from 0.3984375 to 1.59375
Outputs:
- attended: bfloat16 [4, 16384], P(None, ('kvh', 'seq'))
- normed: bfloat16 [4, 16384], P(None, ('kvh', 'seq'))
All inputs are finite; a program needn't handle non-finite values.
Results may differ from a plain program's by a relative error of at most 0.006.
Values may be sent and summed in bfloat16 or wider, within the bound.
A program may use at most 64 MiB of HBM per device.

v0:
```python
import jax
import jax.numpy as jnp
from jax import lax
from jax.sharding import PartitionSpec as P


def merged(shard, axis, combine):
    everything = jax.tree.map(lambda part: lax.all_gather(part, axis), shard)
    leading = jax.tree.map(lambda part: part[0], everything)

    def lap(k, so_far):
        return combine(so_far, jax.tree.map(lambda part: part[k], everything))

    return lax.fori_loop(1, lax.axis_size(axis), lap, leading)


def softmax_pair(first, second):
    highest = jnp.maximum(first[0], second[0])
    first_scale = jnp.exp(first[0] - highest)
    second_scale = jnp.exp(second[0] - highest)
    weight_total = first[1] * first_scale + second[1] * second_scale
    output_total = first[2] * first_scale[..., None] + second[2] * second_scale[..., None]
    return (highest, weight_total, output_total)


def body(queries, keys, values, lengths, hidden_in, out_weight, norm_gain):
    rows, heads_here, head_dim = queries.shape
    groups = keys.shape[1]
    positions = keys.shape[2]
    per_group = heads_here // groups
    query_grid = queries.reshape(rows, groups, per_group, head_dim)
    scores = jnp.einsum(
        "rkgd,rktd->rkgt", query_grid, keys, preferred_element_type=jnp.float32
    ) * head_dim ** (-0.5)
    valid = (jnp.arange(positions, dtype=jnp.int32)[None, :] < lengths)[:, None, None, :]
    peak_here = jnp.max(jnp.where(valid, scores, -jnp.inf), axis=-1)
    probs = jnp.exp(jnp.where(valid, scores - peak_here[..., None], -jnp.inf)).astype(jnp.bfloat16)
    weight_here = jnp.sum(probs, axis=-1, dtype=jnp.float32)
    partial_value = jnp.einsum("rkgt,rktd->rkgd", probs, values, preferred_element_type=jnp.float32)
    feature_width = heads_here * head_dim // lax.axis_size("seq")
    feature_start = lax.axis_index("seq") * feature_width
    highest, weight_total, output_total = merged(
        (peak_here, weight_here, partial_value), "seq", softmax_pair
    )
    whole_out = (output_total / weight_total[..., None]).reshape(rows, heads_here * head_dim)
    attention = lax.dynamic_slice_in_dim(whole_out, feature_start, feature_width, 1)
    attention = attention.astype(jnp.bfloat16)
    projected = jnp.dot(attention, out_weight, preferred_element_type=jnp.float32)
    slice_width = hidden_in.shape[1]
    slice_start = lax.axis_index(("kvh", "seq")) * slice_width
    gain_wide = norm_gain.astype(jnp.float32)
    projected_all = lax.psum(projected, ("kvh", "seq"))
    residual = lax.all_gather(hidden_in, ("kvh", "seq"), axis=1, tiled=True)
    stream_all = (residual.astype(jnp.float32) + projected_all).astype(jnp.bfloat16)
    stream_wide = stream_all.astype(jnp.float32)
    mean_square = jnp.mean(stream_wide * stream_wide, axis=1, keepdims=True)
    normed_all = (stream_wide * lax.rsqrt(mean_square + 1e-05) * gain_wide[None, :]).astype(
        jnp.bfloat16
    )
    attended = lax.dynamic_slice_in_dim(stream_all, slice_start, slice_width, 1)
    normed = lax.dynamic_slice_in_dim(normed_all, slice_start, slice_width, 1)
    return (attended, normed)


def solution(mesh):
    placed = (
        P(None, "kvh", None),
        P(None, "kvh", "seq", None),
        P(None, "kvh", "seq", None),
        P(None, "seq"),
        P(None, ("kvh", "seq")),
        P(("kvh", "seq"), None),
        P(),
    )
    return jax.shard_map(
        body,
        mesh=mesh,
        in_specs=placed,
        out_specs=(P(None, ("kvh", "seq")), P(None, ("kvh", "seq"))),
        check_vma=False,
    )
```

profile of v0, /device:TPU:0, one launch (start us, length us, event | category | flops | bytes accessed | tf_op | source)
XLA Modules:
  0.0 202.7 jit_solution(11224662813829926813)
XLA Ops:
  7.2 0.0 copy-start
  7.2 0.0 copy-start.1
  7.2 0.0 all-reduce.2.cloned.1.call-start
  7.2 0.8 iota_compare_fusion
  8.0 0.1 copy-done
  8.1 1.1 select_reduce_fusion
  9.2 15.8 %all-gather = f32[32,2,16]{2,1,0:T(2,128)S(1)} all-gather(f32[4,2,16]{2,1,0:T(2,128)S(1)} %get-tuple-element.201), channel_id=2, replica_groups=mesh['kvh'=4,'seq'=8] {'seq'}, dimensions={0}, use_global_device_ids=true | all-gather | bytes 4608 | tf_op jit(solution)/shard_map/all_gather | solution.py:8
  25.0 0.2 convert_reduce_fusion
  25.2 1.2 fusion.6
  26.4 14.8 %all-gather.2 = f32[32,2,16,128]{3,2,1,0:T(8,128)S(1)} all-gather(f32[4,2,16,128]{3,2,1,0:T(8,128)S(1)} %fusion.6), channel_id=4, replica_groups=mesh['kvh'=4,'seq'=8] {'seq'}, dimensions={0}, use_global_device_ids=true | all-gather | bytes 589824 | tf_op jit(solution)/shard_map/all_gather | solution.py:8
  41.2 14.2 %all-gather.1 = f32[32,2,16]{2,1,0:T(2,128)S(1)} all-gather(f32[4,2,16]{2,1,0:T(2,128)S(1)} %convert_reduce_fusion), channel_id=3, replica_groups=mesh['kvh'=4,'seq'=8] {'seq'}, dimensions={0}, use_global_device_ids=true | all-gather | bytes 4608 | tf_op jit(solution)/shard_map/all_gather | solution.py:8
  55.4 1.2 while.19
  55.4 0.1 fusion.17
  55.6 0.1 fusion.17
  55.7 0.1 fusion.17
  55.9 0.1 fusion.17
  56.1 0.1 fusion.17
  56.3 0.1 fusion.17
  56.4 0.1 fusion.17
  56.6 0.1 broadcast_divide_fusion
  56.7 8.8 %fusion.5 = f32[4,16384]{1,0:T(4,128)} fusion(bf16[512,16384]{1,0:T(8,128)(2,1)} %param.14, bf16[4,4096]{1,0:T(4,128)(2,1)S(1)} %bitcast.37, s32[]{:T(128)S(6)} %select_n.28), kind=kOutput, calls=%fused_computation.20 | convolution fusion | flops 67108864 | bytes 17043460 | tf_op jit(solution)/shard_map/dot_general | solution.py:48
  65.4 0.0 all-reduce.2.cloned.1.call-update
  65.5 0.8 dynamic-slice
  66.2 0.0 copy-done.1
  66.2 42.1 %all_gather.21 = bf16[4,16384]{1,0:T(4,128)(2,1)S(1)} all-gather(bf16[4,512]{1,0:T(4,128)(2,1)S(1)} %copy-done.1), channel_id=1, replica_groups=mesh['kvh'=4,'seq'=8] {'kvh','seq'}, dimensions={1}, use_global_device_ids=true | all-gather | bytes 135168 | tf_op jit(solution)/shard_map/all_gather | solution.py:53
  108.4 85.0 %all-reduce.2.cloned.1.call-done = f32[4,16384]{1,0:T(4,128)} async-done(((f32[4,16384]{1,0:T(4,128)}), f32[4,16384]{1,0:T(4,128)}) %all-reduce.2.cloned.1.call-update) | async-done | bytes 262160 | tf_op jit(solution)/shard_map/psum | solution.py:52
  193.4 1.2 multiply_reduce_fusion
  194.6 0.6 constant_dynamic-slice_fusion
  195.2 0.7 fusion.4
  (13 shorter events, 0.3 us)
Async XLA Ops:
  7.2 1.0 copy-start
  7.2 59.1 %copy-start.1 = (bf16[4,512]{1,0:T(4,128)(2,1)S(1)}, bf16[4,512]{1,0:T(4,128)(2,1)}, u32[]{:S(2)}) copy-start(bf16[4,512]{1,0:T(4,128)(2,1)} %param.13) | copy-start | bytes 12292
  7.2 186.2 %all-reduce.2.cloned.1.call-start = ((), (), s32[]{:S(2)}) async-start(), calls=%async_computation | async-start | bytes 524288 | tf_op jit(solution)/shard_map/psum | solution.py:52
Sparse Core Ops, SparseCore 0:
  65.6 127.7 all-reduce.1
where the time goes:
time: 203 us
  blocking collectives  86.9 us (43%)
  waiting for transfers between devices  85 us (42%)
  between operations  14.1 us (7%)
  matrix products  11 us (5%)
  other arithmetic  3.94 us (2%)
    psum x1, waiting for transfers between devices, body(): projected_all = lax.psum(projected, ('kvh', 'seq'))  85 us
    all_gather x3, blocking collectives, merged(): everything = jax.tree.map(lambda part: lax.all_gather(part, axis), shard)  44.8 us
    all_gather x1, blocking collectives, body(): residual = lax.all_gather(hidden_in, ('kvh', 'seq'), axis=1, tiled=True)  42.1 us
    dot_general x1, matrix products, body(): jnp.dot(attention, out_weight, preferred_element_type=jnp.float32)  8.75 us
  transfers between devices with their start and end apart: 1, of which 1 were waited for; matrix products, arithmetic and copies ran while one was open for 0% of the time, Pallas kernels for 0%

commit v1 on v0

--- a/solution.py
+++ b/solution.py
@@ -2,6 +2,10 @@
 import jax.numpy as jnp
 from jax import lax
 from jax.sharding import PartitionSpec as P
+
+
+def post_panel(device_axis, slab_in):
+    return jnp.sum(jax.lax.all_gather(slab_in, device_axis), 0)
 
 
 def merged(shard, axis, combine):
@@ -49,7 +53,7 @@
     slice_width = hidden_in.shape[1]
     slice_start = lax.axis_index(("kvh", "seq")) * slice_width
     gain_wide = norm_gain.astype(jnp.float32)
-    projected_all = lax.psum(projected, ("kvh", "seq"))
+    projected_all = post_panel(("kvh", "seq"), projected)
     residual = lax.all_gather(hidden_in, ("kvh", "seq"), axis=1, tiled=True)
     stream_all = (residual.astype(jnp.float32) + projected_all).astype(jnp.bfloat16)
     stream_wide = stream_all.astype(jnp.float32)

time: 203 us -> 157 us (0.77)
  waiting for transfers between devices: 85 us -> 35.2 us
  other arithmetic: 3.94 us -> 7.74 us
    psum x1 -> x0, waiting for transfers between devices: 85 us -> none  [body(): projected_all = lax.psum(projected, ('kvh', 'seq'))]
    all_gather x0 -> x1, waiting for transfers between devices: none -> 35.1 us  [post_panel(): return jnp.sum(jax.lax.all_gather(slab_in, device_axis), 0)]
    reduce_sum x0 -> x1, other arithmetic: none -> 4.75 us  [post_panel(): return jnp.sum(jax.lax.all_gather(slab_in, device_axis), 0)]
where the time goes in v1:
time: 157 us
  blocking collectives  87.3 us (56%)
  waiting for transfers between devices  35.2 us (22%)
  between operations  14.1 us (9%)
  matrix products  11 us (7%)
  other arithmetic  7.74 us (5%)
    all_gather x3, blocking collectives, merged(): everything = jax.tree.map(lambda part: lax.all_gather(part, axis), shard)  44.8 us
    all_gather x1, blocking collectives, body(): residual = lax.all_gather(hidden_in, ('kvh', 'seq'), axis=1, tiled=True)  42.5 us
    all_gather x1, waiting for transfers between devices, post_panel(): return jnp.sum(jax.lax.all_gather(slab_in, device_axis), 0)  35.1 us
    dot_general x1, matrix products, body(): jnp.dot(attention, out_weight, preferred_element_type=jnp.float32)  8.76 us
    reduce_sum x1, other arithmetic, post_panel(): return jnp.sum(jax.lax.all_gather(slab_in, device_axis), 0)  4.75 us
  transfers between devices with their start and end apart: 1, of which 1 were waited for; matrix products, arithmetic and copies ran while one was open for 0% of the time, Pallas kernels for 0%

profile of v1, /device:TPU:0, one launch (start us, length us, event | category | flops | bytes accessed | tf_op | source)
XLA Modules:
  0.0 157.1 jit_solution(4504486294759392138)
XLA Ops:
  7.2 0.0 copy-start
  7.2 0.0 copy-start.1
  7.2 0.0 all-gather.7.cloned.1.call-start
  7.2 0.8 iota_compare_fusion
  8.0 0.1 copy-done
  8.1 1.1 select_reduce_fusion
  9.2 15.8 %all-gather = f32[32,2,16]{2,1,0:T(2,128)S(1)} all-gather(f32[4,2,16]{2,1,0:T(2,128)S(1)} %get-tuple-element.201), channel_id=2, replica_groups=mesh['kvh'=4,'seq'=8] {'seq'}, dimensions={0}, use_global_device_ids=true | all-gather | bytes 4608 | tf_op jit(solution)/shard_map/all_gather | solution.py:12
  25.0 0.2 convert_reduce_fusion
  25.2 1.2 fusion.5
  26.4 14.8 %all-gather.2 = f32[32,2,16,128]{3,2,1,0:T(8,128)S(1)} all-gather(f32[4,2,16,128]{3,2,1,0:T(8,128)S(1)} %fusion.5), channel_id=4, replica_groups=mesh['kvh'=4,'seq'=8] {'seq'}, dimensions={0}, use_global_device_ids=true | all-gather | bytes 589824 | tf_op jit(solution)/shard_map/all_gather | solution.py:12
  41.2 14.2 %all-gather.1 = f32[32,2,16]{2,1,0:T(2,128)S(1)} all-gather(f32[4,2,16]{2,1,0:T(2,128)S(1)} %convert_reduce_fusion), channel_id=3, replica_groups=mesh['kvh'=4,'seq'=8] {'seq'}, dimensions={0}, use_global_device_ids=true | all-gather | bytes 4608 | tf_op jit(solution)/shard_map/all_gather | solution.py:12
  55.4 1.2 while.19
  55.4 0.1 fusion.16
  55.6 0.1 fusion.16
  55.7 0.1 fusion.16
  55.9 0.1 fusion.16
  56.1 0.1 fusion.16
  56.3 0.1 fusion.16
  56.4 0.1 fusion.16
  56.6 0.1 broadcast_divide_fusion
  56.7 8.8 %convolution_bitcast_fusion = f32[1,4,16384]{2,1,0:T(4,128)} fusion(bf16[512,16384]{1,0:T(8,128)(2,1)} %param.14, bf16[4,4096]{1,0:T(4,128)(2,1)S(1)} %bitcast.39, s32[]{:T(128)S(6)} %select_n.28), kind=kOutput, calls=%fused_computation.8 | convolution fusion | flops 67108864 | bytes 17043460 | tf_op jit(solution)/shard_map/dot_general | solution.py:52
  65.4 0.0 all-gather.7.cloned.1.call-update
  65.5 0.8 dynamic-slice
  66.2 0.0 copy-done.1
  66.2 42.5 %all_gather.27 = bf16[4,16384]{1,0:T(4,128)(2,1)S(1)} all-gather(bf16[4,512]{1,0:T(4,128)(2,1)S(1)} %copy-done.1), channel_id=1, replica_groups=mesh['kvh'=4,'seq'=8] {'kvh','seq'}, dimensions={1}, use_global_device_ids=true | all-gather | bytes 135168 | tf_op jit(solution)/shard_map/all_gather | solution.py:57
  108.8 35.1 %all-gather.7.cloned.1.call-done = f32[32,4,16384]{2,1,0:T(4,128)} async-done(((f32[1,4,16384]{2,1,0:T(4,128)}), f32[32,4,16384]{2,1,0:T(4,128)}) %all-gather.7.cloned.1.call-update) | async-done | bytes 8388624 | tf_op jit(solution)/shard_map/all_gather | solution.py:8
  143.9 4.8 %reduce_sum.28 = f32[4,16384]{1,0:T(4,128)S(1)} reduce(f32[32,4,16384]{2,1,0:T(4,128)} %all-gather.7.cloned.1.call-done, f32[]{:T(128)} %constant.56.clone.1), dimensions={0}, to_apply=%region_4.5 | reduce | flops 2031616 | bytes 8650756 | tf_op jit(solution)/shard_map/reduce_sum | solution.py:8
  148.7 0.3 multiply_reduce_fusion
  149.0 0.6 constant_dynamic-slice_fusion
  149.6 0.7 fusion.4
  (13 shorter events, 0.3 us)
Async XLA Ops:
  7.2 1.0 copy-start
  7.2 59.1 %copy-start.1 = (bf16[4,512]{1,0:T(4,128)(2,1)S(1)}, bf16[4,512]{1,0:T(4,128)(2,1)}, u32[]{:S(2)}) copy-start(bf16[4,512]{1,0:T(4,128)(2,1)} %param.13) | copy-start | bytes 12292
  7.2 136.7 %all-gather.7.cloned.1.call-start = ((), (), s32[]{:S(2)}) async-start(), calls=%async_computation | async-start | bytes 8650752 | tf_op jit(solution)/shard_map/all_gather | solution.py:8
Sparse Core Ops, SparseCore 0:
  65.6 78.2 all-gather.6

commit v2 on v0

--- a/solution.py
+++ b/solution.py
@@ -24,6 +24,12 @@
 
 
 def body(queries, keys, values, lengths, hidden_in, out_weight, norm_gain):
+
+    def feed_ports_by_axis(arr_in, ax_name, link_axis):
+        for rr in (link_axis, ax_name):
+            arr_in = lax.psum(arr_in, rr)
+        return arr_in
+
     rows, heads_here, head_dim = queries.shape
     groups = keys.shape[1]
     positions = keys.shape[2]
@@ -49,7 +55,7 @@
     slice_width = hidden_in.shape[1]
     slice_start = lax.axis_index(("kvh", "seq")) * slice_width
     gain_wide = norm_gain.astype(jnp.float32)
-    projected_all = lax.psum(projected, ("kvh", "seq"))
+    projected_all = feed_ports_by_axis(projected, "seq", "kvh")
     residual = lax.all_gather(hidden_in, ("kvh", "seq"), axis=1, tiled=True)
     stream_all = (residual.astype(jnp.float32) + projected_all).astype(jnp.bfloat16)
     stream_wide = stream_all.astype(jnp.float32)

time: 203 us -> 177 us (0.87)
  waiting for transfers between devices: 85 us -> 60.2 us
    psum x1 -> x2, waiting for transfers between devices: 85 us -> 60.2 us  [feed_ports_by_axis(): arr_in = lax.psum(arr_in, rr)]
  transfers between devices with their start and end apart: 1 -> 2, of which waited for: 1 -> 2; matrix products, arithmetic and copies ran while one was open for 0% -> 0% of each run, Pallas kernels for 0% -> 0%
where the time goes in v2:
time: 177 us
  blocking collectives  85.8 us (48%)
  waiting for transfers between devices  60.2 us (34%)
  between operations  14.1 us (8%)
  matrix products  11 us (6%)
  other arithmetic  3.94 us (2%)
    psum x2, waiting for transfers between devices, feed_ports_by_axis(): arr_in = lax.psum(arr_in, rr)  60.2 us
    all_gather x3, blocking collectives, merged(): everything = jax.tree.map(lambda part: lax.all_gather(part, axis), shard)  44.8 us
    all_gather x1, blocking collectives, body(): residual = lax.all_gather(hidden_in, ('kvh', 'seq'), axis=1, tiled=True)  41 us
    dot_general x1, matrix products, body(): jnp.dot(attention, out_weight, preferred_element_type=jnp.float32)  8.75 us
  transfers between devices with their start and end apart: 2, of which 2 were waited for; matrix products, arithmetic and copies ran while one was open for 0% of the time, Pallas kernels for 0%

profile of v2, /device:TPU:0, one launch (start us, length us, event | category | flops | bytes accessed | tf_op | source)
XLA Modules:
  0.0 176.9 jit_solution(7410875265733757859)
XLA Ops:
  7.2 0.0 copy-start
  7.2 0.0 copy-start.1
  7.2 0.0 all-reduce.3.cloned.1.call-start
  7.2 0.8 iota_compare_fusion
  8.0 0.1 copy-done
  8.1 1.1 select_reduce_fusion
  9.2 15.8 %all-gather = f32[32,2,16]{2,1,0:T(2,128)S(1)} all-gather(f32[4,2,16]{2,1,0:T(2,128)S(1)} %get-tuple-element.201), channel_id=2, replica_groups=mesh['kvh'=4,'seq'=8] {'seq'}, dimensions={0}, use_global_device_ids=true | all-gather | bytes 4608 | tf_op jit(solution)/shard_map/all_gather | solution.py:8
  25.0 0.2 convert_reduce_fusion
  25.2 1.2 fusion.6
  26.4 14.8 %all-gather.2 = f32[32,2,16,128]{3,2,1,0:T(8,128)S(1)} all-gather(f32[4,2,16,128]{3,2,1,0:T(8,128)S(1)} %fusion.6), channel_id=4, replica_groups=mesh['kvh'=4,'seq'=8] {'seq'}, dimensions={0}, use_global_device_ids=true | all-gather | bytes 589824 | tf_op jit(solution)/shard_map/all_gather | solution.py:8
  41.2 14.2 %all-gather.1 = f32[32,2,16]{2,1,0:T(2,128)S(1)} all-gather(f32[4,2,16]{2,1,0:T(2,128)S(1)} %convert_reduce_fusion), channel_id=3, replica_groups=mesh['kvh'=4,'seq'=8] {'seq'}, dimensions={0}, use_global_device_ids=true | all-gather | bytes 4608 | tf_op jit(solution)/shard_map/all_gather | solution.py:8
  55.4 1.2 while.19
  55.4 0.1 fusion.17
  55.6 0.1 fusion.17
  55.7 0.1 fusion.17
  55.9 0.1 fusion.17
  56.1 0.1 fusion.17
  56.3 0.1 fusion.17
  56.4 0.1 fusion.17
  56.6 0.1 broadcast_divide_fusion
  56.7 8.8 %fusion.5 = f32[4,16384]{1,0:T(4,128)} fusion(bf16[512,16384]{1,0:T(8,128)(2,1)} %param.14, bf16[4,4096]{1,0:T(4,128)(2,1)S(1)} %bitcast.37, s32[]{:T(128)S(6)} %select_n.28), kind=kOutput, calls=%fused_computation.20 | convolution fusion | flops 67108864 | bytes 17043460 | tf_op jit(solution)/shard_map/dot_general | solution.py:54
  65.4 0.0 all-reduce.3.cloned.1.call-update
  65.5 0.0 all-reduce.5.cloned.1.call-start
  65.5 44.2 %all-reduce.3.cloned.1.call-done = f32[4,16384]{1,0:T(4,128)} async-done(((f32[4,16384]{1,0:T(4,128)}), f32[4,16384]{1,0:T(4,128)}) %all-reduce.3.cloned.1.call-update) | async-done | bytes 262160 | tf_op jit(solution)/shard_map/psum | solution.py:30
  109.8 0.0 all-reduce.5.cloned.1.call-update
  109.8 0.8 dynamic-slice
  110.6 0.0 copy-done.1
  110.6 41.0 %all_gather.21 = bf16[4,16384]{1,0:T(4,128)(2,1)S(1)} all-gather(bf16[4,512]{1,0:T(4,128)(2,1)S(1)} %copy-done.1), channel_id=1, replica_groups=mesh['kvh'=4,'seq'=8] {'kvh','seq'}, dimensions={1}, use_global_device_ids=true | all-gather | bytes 135168 | tf_op jit(solution)/shard_map/all_gather | solution.py:59
  151.6 15.9 %all-reduce.5.cloned.1.call-done = f32[4,16384]{1,0:T(4,128)} async-done(((f32[4,16384]{1,0:T(4,128)}), f32[4,16384]{1,0:T(4,128)}) %all-reduce.5.cloned.1.call-update) | async-done | bytes 262160 | tf_op jit(solution)/shard_map/psum | solution.py:30
  167.5 1.2 multiply_reduce_fusion
  168.8 0.6 constant_dynamic-slice_fusion
  169.4 0.7 fusion.4
  (13 shorter events, 0.3 us)
Async XLA Ops:
  7.2 1.0 copy-start
  7.2 103.4 %copy-start.1 = (bf16[4,512]{1,0:T(4,128)(2,1)S(1)}, bf16[4,512]{1,0:T(4,128)(2,1)}, u32[]{:S(2)}) copy-start(bf16[4,512]{1,0:T(4,128)(2,1)} %param.13) | copy-start | bytes 12292
  7.2 102.6 %all-reduce.3.cloned.1.call-start = ((), (), s32[]{:S(2)}) async-start(), calls=%async_computation | async-start | bytes 524288 | tf_op jit(solution)/shard_map/psum | solution.py:30
  65.5 102.1 %all-reduce.5.cloned.1.call-start = ((), (), s32[]{:S(2)}) async-start(), calls=%async_computation.1 | async-start | bytes 524288 | tf_op jit(solution)/shard_map/psum | solution.py:30
Sparse Core Ops, SparseCore 0:
  65.6 44.1 all-reduce.2
  112.1 55.4 all-reduce.4
